TPU v7x, 32 devices: a whole 2x2x4 slice. The times are simulated.
32 devices in a mesh: dp: 8 (over y, x, core), tensor: 4 (over z).
Axes of the slice: x: 2, y: 2, z: 4, core: 2. Of those that a mesh axis runs over, the one named last changes fastest.
Arguments:
- block_in: bfloat16 [8192, 4096], P(('dp', 'tensor')), may hold values from -6 to 6
- out_grad: bfloat16 [8192, 4096], P(('dp', 'tensor')), may hold values from -6 to 6
- segment_ids: int32 [8192], P('dp'), may hold values from 0 to 2, as said below
- positions: int32 [8192], P('dp'), may hold values from 0 to 1023, as said below
- group_token_counts: int32 [8], P('dp'), may hold values from 512 to 1024, as said below
- gain_attn: float32 [4096], replicated, may hold values from 0.1 to 1.9
- w_query: bfloat16 [4096, 4096], P('dp', 'tensor'), may hold values from -0.3125 to 0.3125
- w_key: bfloat16 [4096, 4096], P('dp', 'tensor'), may hold values from -0.3125 to 0.3125
- w_value: bfloat16 [4096, 4096], P('dp', 'tensor'), may hold values from -0.09375 to 0.09375
- w_out: bfloat16 [4096, 4096], P('tensor', 'dp'), may hold values from -0.5 to 0.5
- gain_mlp: float32 [4096], replicated, may hold values from 0.1 to 1.9
- w_gate: bfloat16 [4096, 11008], P('dp', 'tensor'), may hold values from -0.09375 to 0.09375
- w_up: bfloat16 [4096, 11008], P('dp', 'tensor'), may hold values from -0.09375 to 0.09375
- w_down: bfloat16 [11008, 4096], P('tensor', 'dp'), may hold values from -0.0546875 to 0.0546875
Outputs:
- block_out: bfloat16 [8192, 4096], P(('dp', 'tensor'))
- input_grad: bfloat16 [8192, 4096], P(('dp', 'tensor'))
- grad_gain_attn: float32 [4096], replicated
- grad_query: float32 [4096, 4096], P('dp', 'tensor')
- grad_key: float32 [4096, 4096], P('dp', 'tensor')
- grad_value: float32 [4096, 4096], P('dp', 'tensor')
- grad_out: float32 [4096, 4096], P('tensor', 'dp')
- grad_gain_mlp: float32 [4096], replicated
- grad_gate: float32 [4096, 11008], P('dp', 'tensor')
- grad_up: float32 [4096, 11008], P('dp', 'tensor')
- grad_down: float32 [11008, 4096], P('tensor', 'dp')
Inputs may be any that keep to these rules, and one draw needn't show every extreme that they name: `segment_ids`: within each group of 1024 rows segment ids never fall; ids 0 and 1 are the group's sequences (1 may be absent) and 2 marks the rows from group_token_counts of that group on, when there are any. In a group whose live rows number 1024 or more, sequence 0 holds at least 1024 rows; otherwise it holds all live rows. Each segment's positions run 0, 1, 2, ... in row order. In every draw some group is one sequence of all 1024 rows. `group_token_counts`: some group is full in every draw.
All inputs are finite; a program needn't handle non-finite values.
Results may differ from a plain program's by a relative error of at most 0.014.
Values may be sent and summed in bfloat16 or wider, within the bound.
No kernel may reach another device: no remote copies, remote signals or barrier semaphores. Data moves between devices by JAX's collectives and lax.ppermute only.
A program may use at most 448 MiB of HBM per device.

v0:
```python
import jax
import jax.numpy as jnp
from jax import lax
from jax.sharding import PartitionSpec as P

QBLOCKS = 4
HEAD_DIM = 128
EPSILON = 1e-05
ROPE_BASE = 10000.0


def matmul(left, right):
    return jnp.dot(left, right, preferred_element_type=jnp.float32)


def left_t(left, right):
    return lax.dot_general(
        left, right, (((0,), (0,)), ((), ())), preferred_element_type=jnp.float32
    )


def right_t(left, right):
    return lax.dot_general(
        left, right, (((1,), (1,)), ((), ())), preferred_element_type=jnp.float32
    )


def rope_tables(position):
    half_dim = HEAD_DIM // 2
    freq_index = jnp.arange(half_dim).astype(jnp.float32)
    frequency = ROPE_BASE ** (-2.0 * freq_index / HEAD_DIM)
    angles = position.astype(jnp.float32)[:, None] * frequency[None, :]
    cos_tab = jnp.cos(angles)
    sine_tab = jnp.sin(angles)
    return (
        jnp.concatenate([cos_tab, cos_tab], 1)[:, None, :],
        jnp.concatenate([sine_tab, sine_tab], 1)[:, None, :],
    )


def rotate(field):
    half_dim = field.shape[-1] // 2
    return jnp.concatenate([-field[..., half_dim:], field[..., :half_dim]], -1)


def rotate_back(field):
    half_dim = field.shape[-1] // 2
    return jnp.concatenate([field[..., half_dim:], -field[..., :half_dim]], -1)


def apply_rope(field, cos_tab, sine_tab):
    return field * cos_tab + rotate(field) * sine_tab


def undo_rope(field, cos_tab, sine_tab):
    return field * cos_tab + rotate_back(field * sine_tab)


def norm_back(layer_in, row_inverse_scale, norm_weight, normalized_gradient):
    standardized_gradient = normalized_gradient * norm_weight
    standardized_rows = layer_in * row_inverse_scale
    layer_gradient = row_inverse_scale * (
        standardized_gradient
        - standardized_rows
        * jnp.mean(standardized_gradient * standardized_rows, axis=1, keepdims=True)
    )
    return (layer_gradient, jnp.sum(normalized_gradient * standardized_rows, axis=0))


def shards(
    block_in,
    out_grad,
    segment_ids,
    positions,
    group_token_counts,
    gain_attn,
    w_query,
    w_key,
    w_value,
    w_out,
    gain_mlp,
    w_gate,
    w_up,
    w_down,
):
    tok_rows = block_in.shape[0]
    query_all, key_all, value_all, out_all = (
        lax.all_gather(w_query, "dp", axis=0, tiled=True),
        lax.all_gather(w_key, "dp", axis=0, tiled=True),
        lax.all_gather(w_value, "dp", axis=0, tiled=True),
        lax.all_gather(w_out, "dp", axis=1, tiled=True),
    )
    gate_all, up_all, down_all = (
        lax.all_gather(w_gate, "dp", axis=0, tiled=True),
        lax.all_gather(w_up, "dp", axis=0, tiled=True),
        lax.all_gather(w_down, "dp", axis=1, tiled=True),
    )
    x_float = block_in.astype(jnp.float32)
    attn_scale = lax.rsqrt(jnp.mean(x_float * x_float, axis=1, keepdims=True) + EPSILON)
    attn_normed = (x_float * attn_scale * gain_attn).astype(jnp.bfloat16)
    whole_attn = lax.all_gather(attn_normed, "tensor", axis=0, tiled=True)
    group_rows = whole_attn.shape[0]
    local_heads = query_all.shape[1] // HEAD_DIM
    cos_tab, sine_tab = rope_tables(positions)

    def split_heads(field):
        return field.reshape(group_rows, local_heads, HEAD_DIM)

    queries = apply_rope(split_heads(matmul(whole_attn, query_all)), cos_tab, sine_tab).astype(
        jnp.bfloat16
    )
    keys_all = apply_rope(split_heads(matmul(whole_attn, key_all)), cos_tab, sine_tab).astype(
        jnp.bfloat16
    )
    values = split_heads(matmul(whole_attn, value_all)).astype(jnp.bfloat16)
    block_rows = group_rows // QBLOCKS
    row_order = jnp.arange(group_rows)
    score_scale = HEAD_DIM ** (-0.5)

    def block_scores(block_index):
        low_row = block_index * block_rows
        high_row = low_row + block_rows
        scores = (
            jnp.einsum(
                "qhd,khd->hqk",
                queries[low_row:high_row],
                keys_all[:high_row],
                preferred_element_type=jnp.float32,
            )
            * score_scale
        )
        allowed = (segment_ids[low_row:high_row, None] == segment_ids[None, :high_row]) & (
            row_order[None, :high_row] <= row_order[low_row:high_row, None]
        )
        return jnp.where(allowed[None], scores, -1e30)

    attn_parts = []
    total_parts = []
    for block_index in range(QBLOCKS):
        high_row = (block_index + 1) * block_rows
        scores = block_scores(block_index)
        row_max = jnp.max(scores, axis=2, keepdims=True)
        log_total = row_max + jnp.log(jnp.sum(jnp.exp(scores - row_max), axis=2, keepdims=True))
        prob_bf = jnp.exp(scores - log_total).astype(jnp.bfloat16)
        attn_parts.append(
            jnp.einsum(
                "hqk,khd->qhd", prob_bf, values[:high_row], preferred_element_type=jnp.float32
            ).astype(jnp.bfloat16)
        )
        total_parts.append(log_total)
    attn_heads = jnp.concatenate(attn_parts, 0)
    attn = attn_heads.reshape(group_rows, local_heads * HEAD_DIM)
    resid = x_float + lax.psum_scatter(
        matmul(attn, out_all), "tensor", scatter_dimension=0, tiled=True
    )
    mlp_scale = lax.rsqrt(jnp.mean(resid * resid, axis=1, keepdims=True) + EPSILON)
    mlp_normed = (resid * mlp_scale * gain_mlp).astype(jnp.bfloat16)
    whole_mlp = lax.all_gather(mlp_normed, "tensor", axis=0, tiled=True)
    gate_pre = matmul(whole_mlp, gate_all)
    up_pre = matmul(whole_mlp, up_all)
    sigmoid_gate = jax.nn.sigmoid(gate_pre)
    silu_gate = gate_pre * sigmoid_gate
    hidden = (silu_gate * up_pre).astype(jnp.bfloat16)
    block_out = (
        resid
        + lax.psum_scatter(
            matmul(hidden, down_all).astype(jnp.bfloat16), "tensor", scatter_dimension=0, tiled=True
        ).astype(jnp.float32)
    ).astype(jnp.bfloat16)
    first_live = lax.axis_index("tensor") * tok_rows
    live = (first_live + jnp.arange(tok_rows) < group_token_counts[0]).astype(jnp.bfloat16)
    live_grad = out_grad * live[:, None]
    whole_grad = lax.all_gather(live_grad, "tensor", axis=0, tiled=True)
    d_hidden = right_t(whole_grad, down_all)
    grad_down_part = left_t(hidden, whole_grad)
    d_gate = (d_hidden * up_pre * sigmoid_gate * (1.0 + gate_pre * (1.0 - sigmoid_gate))).astype(
        jnp.bfloat16
    )
    d_up = (d_hidden * silu_gate).astype(jnp.bfloat16)
    grad_gate_part = left_t(whole_mlp, d_gate)
    grad_up_part = left_t(whole_mlp, d_up)
    d_norm_mlp = lax.psum_scatter(
        right_t(d_gate, gate_all) + right_t(d_up, up_all), "tensor", scatter_dimension=0, tiled=True
    )
    d_from_mlp, gain_mlp_part = norm_back(resid, mlp_scale, gain_mlp, d_norm_mlp)
    d_resid = live_grad.astype(jnp.float32) + d_from_mlp
    d_resid_b = d_resid.astype(jnp.bfloat16)
    whole_resid = lax.all_gather(d_resid_b, "tensor", axis=0, tiled=True)
    grad_out_part = left_t(attn, whole_resid)
    d_attn = split_heads(right_t(whole_resid, out_all).astype(jnp.bfloat16))
    d_q_parts = []
    d_key_sum = jnp.zeros((group_rows, local_heads, HEAD_DIM), jnp.float32)
    d_value_sum = jnp.zeros((group_rows, local_heads, HEAD_DIM), jnp.float32)
    for block_index in range(QBLOCKS):
        low_row = block_index * block_rows
        high_row = low_row + block_rows
        scores = block_scores(block_index)
        prob_full = jnp.exp(scores - total_parts[block_index])
        dout_rows = d_attn[low_row:high_row]
        row_delta = jnp.sum(
            dout_rows.astype(jnp.float32) * attn_heads[low_row:high_row].astype(jnp.float32), axis=2
        )
        row_delta = jnp.swapaxes(row_delta, 0, 1)[:, :, None]
        d_probs = jnp.einsum(
            "qhd,khd->hqk", dout_rows, values[:high_row], preferred_element_type=jnp.float32
        )
        d_scores = (prob_full * (d_probs - row_delta) * score_scale).astype(jnp.bfloat16)
        d_value_sum = d_value_sum.at[:high_row].add(
            jnp.einsum(
                "hqk,qhd->khd",
                prob_full.astype(jnp.bfloat16),
                dout_rows,
                preferred_element_type=jnp.float32,
            )
        )
        d_q_parts.append(
            jnp.einsum(
                "hqk,khd->qhd", d_scores, keys_all[:high_row], preferred_element_type=jnp.float32
            )
        )
        d_key_sum = d_key_sum.at[:high_row].add(
            jnp.einsum(
                "hqk,qhd->khd",
                d_scores,
                queries[low_row:high_row],
                preferred_element_type=jnp.float32,
            )
        )
    local_width = local_heads * HEAD_DIM
    d_queries = (
        undo_rope(jnp.concatenate(d_q_parts, 0), cos_tab, sine_tab)
        .astype(jnp.bfloat16)
        .reshape(group_rows, local_width)
    )
    d_keys = (
        undo_rope(d_key_sum, cos_tab, sine_tab)
        .astype(jnp.bfloat16)
        .reshape(group_rows, local_width)
    )
    d_values = d_value_sum.astype(jnp.bfloat16).reshape(group_rows, local_width)
    grad_query_part = left_t(whole_attn, d_queries)
    grad_key_part = left_t(whole_attn, d_keys)
    grad_value_part = left_t(whole_attn, d_values)
    d_norm_attn = lax.psum_scatter(
        right_t(d_queries, query_all) + right_t(d_keys, key_all) + right_t(d_values, value_all),
        "tensor",
        scatter_dimension=0,
        tiled=True,
    )
    d_from_attn, gain_attn_part = norm_back(x_float, attn_scale, gain_attn, d_norm_attn)
    input_grad = (d_resid + d_from_attn).astype(jnp.bfloat16)
    grad_query, grad_key, grad_value, grad_out, grad_gate, grad_up, grad_down = (
        lax.psum_scatter(grad_query_part, "dp", scatter_dimension=0, tiled=True),
        lax.psum_scatter(grad_key_part, "dp", scatter_dimension=0, tiled=True),
        lax.psum_scatter(grad_value_part, "dp", scatter_dimension=0, tiled=True),
        lax.psum_scatter(grad_out_part, "dp", scatter_dimension=1, tiled=True),
        lax.psum_scatter(grad_gate_part, "dp", scatter_dimension=0, tiled=True),
        lax.psum_scatter(grad_up_part, "dp", scatter_dimension=0, tiled=True),
        lax.psum_scatter(grad_down_part, "dp", scatter_dimension=1, tiled=True),
    )
    grad_gain_attn, grad_gain_mlp = lax.psum((gain_attn_part, gain_mlp_part), ("dp", "tensor"))
    return (
        block_out,
        input_grad,
        grad_gain_attn,
        grad_query,
        grad_key,
        grad_value,
        grad_out,
        grad_gain_mlp,
        grad_gate,
        grad_up,
        grad_down,
    )


def solution(mesh):
    placed = (
        P(("dp", "tensor"), None),
        P(("dp", "tensor"), None),
        P("dp"),
        P("dp"),
        P("dp"),
        P(),
        P("dp", "tensor"),
        P("dp", "tensor"),
        P("dp", "tensor"),
        P("tensor", "dp"),
        P(),
        P("dp", "tensor"),
        P("dp", "tensor"),
        P("tensor", "dp"),
    )
    return jax.shard_map(
        shards,
        mesh=mesh,
        in_specs=placed,
        out_specs=(
            P(("dp", "tensor"), None),
            P(("dp", "tensor"), None),
            P(),
            P("dp", "tensor"),
            P("dp", "tensor"),
            P("dp", "tensor"),
            P("tensor", "dp"),
            P(),
            P("dp", "tensor"),
            P("dp", "tensor"),
            P("tensor", "dp"),
        ),
        check_vma=False,
    )
```

profile of v0, /device:TPU:0, one launch (start us, length us, event | category | flops | bytes accessed | tf_op | source)
XLA Modules:
  0.0 3740.4 jit_solution(11734040073000018754)
XLA Ops:
  22.3 143.7 %all-gather.12.cloned.1.call-done = bf16[1024,4096]{1,0:T(8,128)(2,1)} async-done(((bf16[256,4096]{1,0:T(8,128)(2,1)}), bf16[1024,4096]{1,0:T(8,128)(2,1)}) %all-gather.12.cloned.1.call-update) | async-done | bytes 8388624 | tf_op jit(solution)/shard_map/all_gather | solution.py:101
  166.0 54.5 %all-gather.14.cloned.1.call-done = bf16[4096,1024]{1,0:T(8,128)(2,1)} async-done(((bf16[512,1024]{1,0:T(8,128)(2,1)}), bf16[4096,1024]{1,0:T(8,128)(2,1)}) %all-gather.14.cloned.1.call-update) | async-done | bytes 8388624 | tf_op jit(solution)/shard_map/all_gather | solution.py:90
  237.1 39.7 %all-gather.16.cloned.1.call-done = bf16[4096,1024]{1,0:T(8,128)(2,1)} async-done(((bf16[512,1024]{1,0:T(8,128)(2,1)}), bf16[4096,1024]{1,0:T(8,128)(2,1)}) %all-gather.16.cloned.1.call-update) | async-done | bytes 8388624 | tf_op jit(solution)/shard_map/all_gather | solution.py:88
  297.2 35.8 all-gather.18.cloned.1.call-done
  406.3 279.6 %reduce-scatter.12.cloned.1.call-done = f32[256,4096]{1,0:T(8,128)} async-done(((f32[1024,4096]{1,0:T(8,128)}), f32[256,4096]{1,0:T(8,128)}) %reduce-scatter.12.cloned.1.call-update) | async-done | bytes 4194320 | tf_op jit(solution)/shard_map/reduce_scatter | solution.py:153
  697.1 110.3 %all-gather.24.cloned.1.call-done = bf16[4096,2752]{0,1:T(8,128)(2,1)} async-done(((bf16[512,2752]{0,1:T(8,128)(2,1)}), bf16[4096,2752]{0,1:T(8,128)(2,1)}) %all-gather.24.cloned.1.call-update) | async-done | bytes 22544400 | tf_op jit(solution)/shard_map/all_gather | solution.py:94
  807.4 151.9 %all-gather.22.cloned.1.call-done = bf16[1024,4096]{1,0:T(8,128)(2,1)} async-done(((bf16[256,4096]{1,0:T(8,128)(2,1)}), bf16[1024,4096]{1,0:T(8,128)(2,1)}) %all-gather.22.cloned.1.call-update) | async-done | bytes 8388624 | tf_op jit(solution)/shard_map/all_gather | solution.py:158
  990.1 88.2 %all-gather.26.cloned.1.call-done = bf16[4096,2752]{0,1:T(8,128)(2,1)} async-done(((bf16[512,2752]{0,1:T(8,128)(2,1)}), bf16[4096,2752]{0,1:T(8,128)(2,1)}) %all-gather.26.cloned.1.call-update) | async-done | bytes 22544400 | tf_op jit(solution)/shard_map/all_gather | solution.py:95
  1108.9 121.1 %all-gather.30.cloned.1.call-done = bf16[1024,4096]{1,0:T(8,128)(2,1)} async-done(((bf16[256,4096]{1,0:T(8,128)(2,1)}), bf16[1024,4096]{1,0:T(8,128)(2,1)}) %all-gather.30.cloned.1.call-update) | async-done | bytes 8388624 | tf_op jit(solution)/shard_map/all_gather | solution.py:173
  1230.0 119.0 %all-gather.28.cloned.1.call-done = bf16[2752,4096]{1,0:T(8,128)(2,1)} async-done(((bf16[2752,512]{1,0:T(8,128)(2,1)}), bf16[2752,4096]{1,0:T(8,128)(2,1)}) %all-gather.28.cloned.1.call-update) | async-done | bytes 22544400 | tf_op jit(solution)/shard_map/all_gather | solution.py:96
  1349.0 38.0 %multiply_convert_fusion = (bf16[1024,2752]{0,1:T(8,128)(2,1)}, bf16[1024,2752]{0,1:T(8,128)(2,1)}, bf16[1024,2752]{0,1:T(8,128)(2,1)}) fusion(f32[1024,2752]{0,1:T(8,128)} %fusion.75, f32[1024,2752]{0,1:T(8,128)} %fusion.76, bf16[1024,4096]{1,0:T(8,128)(2,1)} %all-gather.30.cloned.1.call-done, bf16[2752,4096]{1,0:T(8,128)(2,1)} %all-gather.28.cloned.1.call-done), kind=kOutput, calls=%fused_computation.1 | convolution fusion | flops 23127719936 | bytes 70385664 | tf_op jit(solution)/shard_map/dot_general | solution.py:23
  1417.1 32.0 convolution_add_fusion
  1449.2 280.4 %reduce-scatter.16.cloned.1.call-done = f32[256,4096]{1,0:T(8,128)} async-done(((f32[1024,4096]{1,0:T(8,128)}), f32[256,4096]{1,0:T(8,128)}) %reduce-scatter.16.cloned.1.call-update) | async-done | bytes 4194320 | tf_op jit(solution)/shard_map/reduce_scatter | solution.py:182
  1739.5 149.5 %all-gather.32.cloned.1.call-done = bf16[1024,4096]{1,0:T(8,128)(2,1)} async-done(((bf16[256,4096]{1,0:T(8,128)(2,1)}), bf16[1024,4096]{1,0:T(8,128)(2,1)}) %all-gather.32.cloned.1.call-update) | async-done | bytes 8388624 | tf_op jit(solution)/shard_map/all_gather | solution.py:188
  2225.0 86.5 %reduce-scatter.18.cloned.1.call-done = f32[256,4096]{1,0:T(8,128)} async-done(((f32[1024,4096]{1,0:T(8,128)}), f32[256,4096]{1,0:T(8,128)}) %reduce-scatter.18.cloned.1.call-update) | async-done | bytes 4194320 | tf_op jit(solution)/shard_map/reduce_scatter | solution.py:244
  2314.9 46.8 %all-reduce.2 = (f32[4096]{0:T(1024)}, f32[4096]{0:T(1024)}) all-reduce(f32[4096]{0:T(1024)S(1)} %get-tuple-element.125, f32[4096]{0:T(1024)S(1)} %copy-done.65), channel_id=1, replica_groups=mesh['dp'=8,'tensor'=4] {'dp','tensor'}, use_global_device_ids=true, to_apply=%region_21.22 | all-reduce | flops 8192 | bytes 65536 | tf_op jit(solution)/shard_map/psum | solution.py:261
  2361.7 98.3 %reduce-scatter.14.cloned.1.call-done = bf16[256,4096]{1,0:T(8,128)(2,1)} async-done(((bf16[1024,4096]{1,0:T(8,128)(2,1)}), bf16[256,4096]{1,0:T(8,128)(2,1)}) %reduce-scatter.14.cloned.1.call-update) | async-done | bytes 2097168 | tf_op jit(solution)/shard_map/reduce_scatter | solution.py:166
  2468.7 255.4 %reduce-scatter.28.cloned.1.call-done = f32[512,2752]{0,1:T(8,128)} async-done(((f32[4096,2752]{0,1:T(8,128)}), f32[512,2752]{0,1:T(8,128)}) %reduce-scatter.28.cloned.1.call-update) | async-done | bytes 5636112 | tf_op jit(solution)/shard_map/reduce_scatter | solution.py:257
  2724.1 263.4 %reduce-scatter.30.cloned.1.call-done = f32[512,2752]{0,1:T(8,128)} async-done(((f32[4096,2752]{0,1:T(8,128)}), f32[512,2752]{0,1:T(8,128)}) %reduce-scatter.30.cloned.1.call-update) | async-done | bytes 5636112 | tf_op jit(solution)/shard_map/reduce_scatter | solution.py:258
  2987.5 263.5 %reduce-scatter.32.cloned.1.call-done = f32[2752,512]{1,0:T(8,128)} async-done(((f32[2752,4096]{1,0:T(8,128)}), f32[2752,512]{1,0:T(8,128)}) %reduce-scatter.32.cloned.1.call-update) | async-done | bytes 5636112 | tf_op jit(solution)/shard_map/reduce_scatter | solution.py:259
  3251.0 120.6 %reduce-scatter.24.cloned.1.call-done = f32[512,1024]{1,0:T(8,128)} async-done(((f32[4096,1024]{1,0:T(8,128)}), f32[512,1024]{1,0:T(8,128)}) %reduce-scatter.24.cloned.1.call-update) | async-done | bytes 2097168 | tf_op jit(solution)/shard_map/reduce_scatter | solution.py:255
  3371.6 120.4 %reduce-scatter.22.cloned.1.call-done = f32[512,1024]{1,0:T(8,128)} async-done(((f32[4096,1024]{1,0:T(8,128)}), f32[512,1024]{1,0:T(8,128)}) %reduce-scatter.22.cloned.1.call-update) | async-done | bytes 2097168 | tf_op jit(solution)/shard_map/reduce_scatter | solution.py:254
  3492.0 120.6 %reduce-scatter.26.cloned.1.call-done = f32[1024,512]{1,0:T(8,128)} async-done(((f32[1024,4096]{1,0:T(8,128)}), f32[1024,512]{1,0:T(8,128)}) %reduce-scatter.26.cloned.1.call-update) | async-done | bytes 2097168 | tf_op jit(solution)/shard_map/reduce_scatter | solution.py:256
  3612.5 120.6 %reduce-scatter.20.cloned.1.call-done = f32[512,1024]{1,0:T(8,128)} async-done(((f32[4096,1024]{1,0:T(8,128)}), f32[512,1024]{1,0:T(8,128)}) %reduce-scatter.20.cloned.1.call-update) | async-done | bytes 2097168 | tf_op jit(solution)/shard_map/reduce_scatter | solution.py:253
  (335 shorter events, 584.1 us)
Async XLA Ops:
  7.2 158.8 %all-gather.12.cloned.1.call-start = ((), (), s32[]{:S(2)}) async-start(), calls=%async_computation.11 | async-start | bytes 10485760 | tf_op jit(solution)/shard_map/all_gather | solution.py:101
  13.5 207.0 %all-gather.14.cloned.1.call-start = ((), (), s32[]{:S(2)}) async-start(), calls=%async_computation.12 | async-start | bytes 9437184 | tf_op jit(solution)/shard_map/all_gather | solution.py:90
  14.2 262.6 %all-gather.16.cloned.1.call-start = ((), (), s32[]{:S(2)}) async-start(), calls=%async_computation.13 | async-start | bytes 9437184 | tf_op jit(solution)/shard_map/all_gather | solution.py:88
  15.0 318.0 %all-gather.18.cloned.1.call-start = ((), (), s32[]{:S(2)}) async-start(), calls=%async_computation.14 | async-start | bytes 9437184 | tf_op jit(solution)/shard_map/all_gather | solution.py:89
  15.5 375.2 %all-gather.20.cloned.1.call-start = ((), (), s32[]{:S(2)}) async-start(), calls=%async_computation.15 | async-start | bytes 9437184 | tf_op jit(solution)/shard_map/all_gather | solution.py:91
  16.1 669.8 %reduce-scatter.12.cloned.1.call-start = ((), (), s32[]{:S(2)}) async-start(), calls=%async_computation.16 | async-start | bytes 20971520 | tf_op jit(solution)/shard_map/reduce_scatter | solution.py:153
  20.2 341.8 %copy-start.20 = (f32[1024,128]{1,0:T(8,128)}, f32[1024,128]{1,0:T(8,128)S(1)}, u32[]{:S(2)}) copy-start(f32[1024,128]{1,0:T(8,128)S(1)} %get-tuple-element.171) | copy-start | bytes 1572868
  20.2 341.8 %copy-start.30 = (f32[1024,128]{1,0:T(8,128)}, f32[1024,128]{1,0:T(8,128)S(1)}, u32[]{:S(2)}) copy-start(f32[1024,128]{1,0:T(8,128)S(1)} %get-tuple-element.172) | copy-start | bytes 1572868
  405.5 401.9 %all-gather.24.cloned.1.call-start = ((), (), s32[]{:S(2)}) async-start(), calls=%async_computation.18 | async-start | bytes 25362432 | tf_op jit(solution)/shard_map/all_gather | solution.py:94
  406.3 553.0 %all-gather.22.cloned.1.call-start = ((), (), s32[]{:S(2)}) async-start(), calls=%async_computation.17 | async-start | bytes 10485760 | tf_op jit(solution)/shard_map/all_gather | solution.py:158
  692.7 385.6 %all-gather.26.cloned.1.call-start = ((), (), s32[]{:S(2)}) async-start(), calls=%async_computation.19 | async-start | bytes 25362432 | tf_op jit(solution)/shard_map/all_gather | solution.py:95
  693.4 536.6 %all-gather.30.cloned.1.call-start = ((), (), s32[]{:S(2)}) async-start(), calls=%async_computation.22 | async-start | bytes 10485760 | tf_op jit(solution)/shard_map/all_gather | solution.py:173
  696.3 652.7 %all-gather.28.cloned.1.call-start = ((), (), s32[]{:S(2)}) async-start(), calls=%async_computation.20 | async-start | bytes 25362432 | tf_op jit(solution)/shard_map/all_gather | solution.py:96
  697.0 1032.6 %reduce-scatter.16.cloned.1.call-start = ((), (), s32[]{:S(2)}) async-start(), calls=%async_computation.23 | async-start | bytes 20971520 | tf_op jit(solution)/shard_map/reduce_scatter | solution.py:182
  1449.2 439.8 %all-gather.32.cloned.1.call-start = ((), (), s32[]{:S(2)}) async-start(), calls=%async_computation.24 | async-start | bytes 10485760 | tf_op jit(solution)/shard_map/all_gather | solution.py:188
  1738.5 573.0 %reduce-scatter.18.cloned.1.call-start = ((), (), s32[]{:S(2)}) async-start(), calls=%async_computation.25 | async-start | bytes 20971520 | tf_op jit(solution)/shard_map/reduce_scatter | solution.py:244
  2032.8 427.2 %reduce-scatter.14.cloned.1.call-start = ((), (), s32[]{:S(2)}) async-start(), calls=%async_computation.21 | async-start | bytes 10485760 | tf_op jit(solution)/shard_map/reduce_scatter | solution.py:166
  2064.4 659.7 %reduce-scatter.28.cloned.1.call-start = ((), (), s32[]{:S(2)}) async-start(), calls=%async_computation.30 | async-start | bytes 50724864 | tf_op jit(solution)/shard_map/reduce_scatter | solution.py:257
  2096.1 891.5 %reduce-scatter.30.cloned.1.call-start = ((), (), s32[]{:S(2)}) async-start(), calls=%async_computation.31 | async-start | bytes 50724864 | tf_op jit(solution)/shard_map/reduce_scatter | solution.py:258
  2128.0 1123.0 %reduce-scatter.32.cloned.1.call-start = ((), (), s32[]{:S(2)}) async-start(), calls=%async_computation.32 | async-start | bytes 50724864 | tf_op jit(solution)/shard_map/reduce_scatter | solution.py:259
  2159.7 1211.9 %reduce-scatter.24.cloned.1.call-start = ((), (), s32[]{:S(2)}) async-start(), calls=%async_computation.28 | async-start | bytes 18874368 | tf_op jit(solution)/shard_map/reduce_scatter | solution.py:255
  2176.1 1315.9 %reduce-scatter.22.cloned.1.call-start = ((), (), s32[]{:S(2)}) async-start(), calls=%async_computation.27 | async-start | bytes 18874368 | tf_op jit(solution)/shard_map/reduce_scatter | solution.py:254
  2192.4 1420.2 %reduce-scatter.26.cloned.1.call-start = ((), (), s32[]{:S(2)}) async-start(), calls=%async_computation.29 | async-start | bytes 18874368 | tf_op jit(solution)/shard_map/reduce_scatter | solution.py:256
  2208.7 1524.4 %reduce-scatter.20.cloned.1.call-start = ((), (), s32[]{:S(2)}) async-start(), calls=%async_computation.26 | async-start | bytes 18874368 | tf_op jit(solution)/shard_map/reduce_scatter | solution.py:253
  (88 other events, 3409.0 us)
Sparse Core Ops, SparseCore 0:
  13.6 152.3 all-gather.11
  167.8 52.6 all-gather.13
  222.4 54.3 all-gather.15
  278.6 54.3 all-gather.17
  334.7 55.9 all-gather.19
  405.6 280.2 reduce-scatter.11
  688.0 119.3 all-gather.23
  809.6 149.6 all-gather.21
  961.3 116.8 all-gather.25
  1080.3 149.6 all-gather.29
  1232.0 116.8 all-gather.27
  1449.3 280.2 reduce-scatter.15
  1738.6 150.3 all-gather.31
  2032.9 278.5 reduce-scatter.17
  2313.8 146.1 reduce-scatter.13
  2464.6 259.4 reduce-scatter.27
  2728.7 258.7 reduce-scatter.29
  2992.2 258.7 reduce-scatter.31
  3255.6 115.9 reduce-scatter.23
  3376.0 115.9 reduce-scatter.21
  3496.5 115.9 reduce-scatter.25
  3617.1 115.9 reduce-scatter.19
where the time goes:
time: 3750 us; the launch traced here: 3740 us
  waiting for transfers between devices  3030 us (81%)
  matrix products  521 us (14%)
  other arithmetic  75.1 us (2%)
  local copies, waits for them, and re-layouts  50.8 us (1%)
  blocking collectives  46.8 us (1%)
    reduce_scatter x1, waiting for transfers between devices, shards(): lax.psum_scatter(right_t(d_gate, gate_all) + right_t(d_up, up_all), 'tens...  280 us
    reduce_scatter x1, waiting for transfers between devices, shards(): lax.psum_scatter(matmul(attn, out_all), 'tensor', scatter_dimension=0, ti...  280 us
    reduce_scatter x1, waiting for transfers between devices, shards(): lax.psum_scatter(grad_down_part, 'dp', scatter_dimension=1, tiled=True)  263 us
    reduce_scatter x1, waiting for transfers between devices, shards(): lax.psum_scatter(grad_up_part, 'dp', scatter_dimension=0, tiled=True)  263 us
    reduce_scatter x1, waiting for transfers between devices, shards(): lax.psum_scatter(grad_gate_part, 'dp', scatter_dimension=0, tiled=True)  255 us
    dot_general x7, matrix products, right_t(): lax.dot_general(left, right, (((1,), (1,)), ((), ())), preferred_element_...  166 us
    dot_general x7, matrix products, left_t(): lax.dot_general(left, right, (((0,), (0,)), ((), ())), preferred_element_...  154 us
    dot_general x7, matrix products, matmul(): return jnp.dot(left, right, preferred_element_type=jnp.float32)  152 us
  transfers between devices with their start and end apart: 22, of which 22 were waited for; matrix products, arithmetic and copies ran while one was open for 10% of the time, Pallas kernels for 0%

commit v1 on v0

--- a/solution.py
+++ b/solution.py
@@ -170,7 +170,14 @@
     first_live = lax.axis_index("tensor") * tok_rows
     live = (first_live + jnp.arange(tok_rows) < group_token_counts[0]).astype(jnp.bfloat16)
     live_grad = out_grad * live[:, None]
-    whole_grad = lax.all_gather(live_grad, "tensor", axis=0, tiled=True)
+    ring = [live_grad]
+    for hop in range(3):
+        ring.append(lax.ppermute(ring[-1], "tensor", [(dev, (dev + 1) % 4) for dev in range(4)]))
+    whole_grad = jnp.roll(
+        jnp.concatenate(ring[::-1], axis=0),
+        (lax.axis_index("tensor") + 1) * ring[0].shape[0],
+        axis=0,
+    )
     d_hidden = right_t(whole_grad, down_all)
     grad_down_part = left_t(hidden, whole_grad)
     d_gate = (d_hidden * up_pre * sigmoid_gate * (1.0 + gate_pre * (1.0 - sigmoid_gate))).astype(

time: 3750 us -> 3630 us (0.968)
  waiting for transfers between devices: 3030 us -> 2880 us
    ppermute x0 -> x3, waiting for transfers between devices: none -> 165 us  [shards(): lax.ppermute(ring[-1], 'tensor', [(dev, (dev + 1) % 4) for dev in range(4)])]
    all_gather x1 -> x0, waiting for transfers between devices: 121 us -> none  [shards(): whole_grad = lax.all_gather(live_grad, 'tensor', axis=0, tiled=True)]
    all_gather x1, waiting for transfers between devices: 110 us -> 0.01 us  [shards(): lax.all_gather(w_gate, 'dp', axis=0, tiled=True)]
    all_gather x1, waiting for transfers between devices: 152 us -> 95.4 us  [shards(): whole_mlp = lax.all_gather(mlp_normed, 'tensor', axis=0, tiled=True)]
  transfers between devices with their start and end apart: 22 -> 24, of which waited for: 22 -> 23; matrix products, arithmetic and copies ran while one was open for 10% -> 11% of each run, Pallas kernels for 0% -> 0%
where the time goes in v1:
time: 3630 us; the launch traced here: 3620 us
  waiting for transfers between devices  2880 us (79%)
  matrix products  533 us (15%)
  other arithmetic  76.6 us (2%)
  local copies, waits for them, and re-layouts  70.5 us (2%)
  blocking collectives  46.8 us (1%)
    reduce_scatter x1, waiting for transfers between devices, shards(): lax.psum_scatter(right_t(d_gate, gate_all) + right_t(d_up, up_all), 'tens...  280 us
    reduce_scatter x1, waiting for transfers between devices, shards(): lax.psum_scatter(matmul(attn, out_all), 'tensor', scatter_dimension=0, ti...  280 us
    reduce_scatter x1, waiting for transfers between devices, shards(): lax.psum_scatter(grad_up_part, 'dp', scatter_dimension=0, tiled=True)  263 us
    reduce_scatter x1, waiting for transfers between devices, shards(): lax.psum_scatter(grad_down_part, 'dp', scatter_dimension=1, tiled=True)  263 us
    reduce_scatter x1, waiting for transfers between devices, shards(): lax.psum_scatter(grad_gate_part, 'dp', scatter_dimension=0, tiled=True)  255 us
    dot_general x7, matrix products, right_t(): lax.dot_general(left, right, (((1,), (1,)), ((), ())), preferred_element_...  166 us
    ppermute x3, waiting for transfers between devices, shards(): lax.ppermute(ring[-1], 'tensor', [(dev, (dev + 1) % 4) for dev in range(4)])  165 us
    dot_general x7, matrix products, left_t(): lax.dot_general(left, right, (((0,), (0,)), ((), ())), preferred_element_...  154 us
  transfers between devices with their start and end apart: 24, of which 23 were waited for; matrix products, arithmetic and copies ran while one was open for 11% of the time, Pallas kernels for 0%

profile of v1, /device:TPU:0, one launch (start us, length us, event | category | flops | bytes accessed | tf_op | source)
XLA Modules:
  0.0 3621.6 jit_solution(9737265911925905987)
XLA Ops:
  22.3 143.6 %all-gather.11.cloned.1.call-done = bf16[1024,4096]{1,0:T(8,128)(2,1)} async-done(((bf16[256,4096]{1,0:T(8,128)(2,1)}), bf16[1024,4096]{1,0:T(8,128)(2,1)}) %all-gather.11.cloned.1.call-update) | async-done | bytes 8388624 | tf_op jit(solution)/shard_map/all_gather | solution.py:101
  166.0 54.5 %all-gather.13.cloned.1.call-done = bf16[4096,1024]{1,0:T(8,128)(2,1)} async-done(((bf16[512,1024]{1,0:T(8,128)(2,1)}), bf16[4096,1024]{1,0:T(8,128)(2,1)}) %all-gather.13.cloned.1.call-update) | async-done | bytes 8388624 | tf_op jit(solution)/shard_map/all_gather | solution.py:90
  237.5 39.3 %all-gather.15.cloned.1.call-done = bf16[4096,1024]{1,0:T(8,128)(2,1)} async-done(((bf16[512,1024]{1,0:T(8,128)(2,1)}), bf16[4096,1024]{1,0:T(8,128)(2,1)}) %all-gather.15.cloned.1.call-update) | async-done | bytes 8388624 | tf_op jit(solution)/shard_map/all_gather | solution.py:88
  297.2 35.8 all-gather.17.cloned.1.call-done
  406.4 279.7 %reduce-scatter.12.cloned.1.call-done = f32[256,4096]{1,0:T(8,128)} async-done(((f32[1024,4096]{1,0:T(8,128)}), f32[256,4096]{1,0:T(8,128)}) %reduce-scatter.12.cloned.1.call-update) | async-done | bytes 4194320 | tf_op jit(solution)/shard_map/reduce_scatter | solution.py:153
  695.1 49.0 %collective-permute-done = bf16[256,4096]{1,0:T(8,128)(2,1)S(1)} collective-permute-done((bf16[256,4096]{1,0:T(8,128)(2,1)S(1)}, bf16[256,4096]{1,0:T(8,128)(2,1)S(1)}, u32[]{:S(2)}, u32[]{:S(2)}) %collective-permute-start) | collective-permute-done | bytes 2097184 | tf_op jit(solution)/shard_map/ppermute | solution.py:175
  745.5 48.2 %collective-permute-done.1 = bf16[256,4096]{1,0:T(8,128)(2,1)} collective-permute-done((bf16[256,4096]{1,0:T(8,128)(2,1)S(1)}, bf16[256,4096]{1,0:T(8,128)(2,1)}, u32[]{:S(2)}, u32[]{:S(2)}) %collective-permute-start.1) | collective-permute-done | bytes 2097184 | tf_op jit(solution)/shard_map/ppermute | solution.py:175
  793.7 68.0 %collective-permute-done.2 = bf16[256,4096]{1,0:T(8,128)(2,1)} collective-permute-done((bf16[256,4096]{1,0:T(8,128)(2,1)}, bf16[256,4096]{1,0:T(8,128)(2,1)}, u32[]{:S(2)}, u32[]{:S(2)}) %collective-permute-start.2) | collective-permute-done | bytes 2097184 | tf_op jit(solution)/shard_map/ppermute | solution.py:175
  881.3 95.4 %all-gather.21.cloned.1.call-done = bf16[1024,4096]{1,0:T(8,128)(2,1)} async-done(((bf16[256,4096]{1,0:T(8,128)(2,1)}), bf16[1024,4096]{1,0:T(8,128)(2,1)}) %all-gather.21.cloned.1.call-update) | async-done | bytes 8388624 | tf_op jit(solution)/shard_map/all_gather | solution.py:158
  1007.9 87.7 %all-gather.25.cloned.1.call-done = bf16[4096,2752]{0,1:T(8,128)(2,1)} async-done(((bf16[512,2752]{0,1:T(8,128)(2,1)}), bf16[4096,2752]{0,1:T(8,128)(2,1)}) %all-gather.25.cloned.1.call-update) | async-done | bytes 22544400 | tf_op jit(solution)/shard_map/all_gather | solution.py:95
  1126.3 89.9 %all-gather.27.cloned.1.call-done = bf16[2752,4096]{1,0:T(8,128)(2,1)} async-done(((bf16[2752,512]{1,0:T(8,128)(2,1)}), bf16[2752,4096]{1,0:T(8,128)(2,1)}) %all-gather.27.cloned.1.call-update) | async-done | bytes 22544400 | tf_op jit(solution)/shard_map/all_gather | solution.py:96
  1216.2 37.7 %multiply_convert_fusion = (bf16[1024,2752]{0,1:T(8,128)(2,1)}, bf16[1024,2752]{0,1:T(8,128)(2,1)}, bf16[1024,2752]{0,1:T(8,128)(2,1)}) fusion(f32[1024,2752]{0,1:T(8,128)} %fusion.81, f32[1024,2752]{0,1:T(8,128)} %fusion.82, bf16[2752,4096]{1,0:T(8,128)(2,1)} %all-gather.27.cloned.1.call-done, bf16[2048,4096]{1,0:T(8,128)(2,1)} %constant_dynamic-update-slice_fusion, ...), kind=kOutput, calls=%fused_computation.1 | convolution fusion | flops 23127719936 | bytes 70385664 | tf_op jit(solution)/shard_map/dot_general | solution.py:23
  1316.0 280.4 %reduce-scatter.16.cloned.1.call-done = f32[256,4096]{1,0:T(8,128)} async-done(((f32[1024,4096]{1,0:T(8,128)}), f32[256,4096]{1,0:T(8,128)}) %reduce-scatter.16.cloned.1.call-update) | async-done | bytes 4194320 | tf_op jit(solution)/shard_map/reduce_scatter | solution.py:189
  1608.6 149.5 %all-gather.29.cloned.1.call-done = bf16[1024,4096]{1,0:T(8,128)(2,1)} async-done(((bf16[256,4096]{1,0:T(8,128)(2,1)}), bf16[1024,4096]{1,0:T(8,128)(2,1)}) %all-gather.29.cloned.1.call-update) | async-done | bytes 8388624 | tf_op jit(solution)/shard_map/all_gather | solution.py:195
  2106.2 86.8 %reduce-scatter.18.cloned.1.call-done = f32[256,4096]{1,0:T(8,128)} async-done(((f32[1024,4096]{1,0:T(8,128)}), f32[256,4096]{1,0:T(8,128)}) %reduce-scatter.18.cloned.1.call-update) | async-done | bytes 4194320 | tf_op jit(solution)/shard_map/reduce_scatter | solution.py:251
  2196.5 46.8 %all-reduce.2 = (f32[4096]{0:T(1024)}, f32[4096]{0:T(1024)}) all-reduce(f32[4096]{0:T(1024)S(1)} %get-tuple-element.125, f32[4096]{0:T(1024)S(1)} %copy-done.77), channel_id=1, replica_groups=mesh['dp'=8,'tensor'=4] {'dp','tensor'}, use_global_device_ids=true, to_apply=%region_21.22 | all-reduce | flops 8192 | bytes 65536 | tf_op jit(solution)/shard_map/psum | solution.py:268
  2243.3 98.3 %reduce-scatter.14.cloned.1.call-done = bf16[256,4096]{1,0:T(8,128)(2,1)} async-done(((bf16[1024,4096]{1,0:T(8,128)(2,1)}), bf16[256,4096]{1,0:T(8,128)(2,1)}) %reduce-scatter.14.cloned.1.call-update) | async-done | bytes 2097168 | tf_op jit(solution)/shard_map/reduce_scatter | solution.py:166
  2350.3 255.4 %reduce-scatter.28.cloned.1.call-done = f32[512,2752]{0,1:T(8,128)} async-done(((f32[4096,2752]{0,1:T(8,128)}), f32[512,2752]{0,1:T(8,128)}) %reduce-scatter.28.cloned.1.call-update) | async-done | bytes 5636112 | tf_op jit(solution)/shard_map/reduce_scatter | solution.py:264
  2605.7 263.5 %reduce-scatter.30.cloned.1.call-done = f32[512,2752]{0,1:T(8,128)} async-done(((f32[4096,2752]{0,1:T(8,128)}), f32[512,2752]{0,1:T(8,128)}) %reduce-scatter.30.cloned.1.call-update) | async-done | bytes 5636112 | tf_op jit(solution)/shard_map/reduce_scatter | solution.py:265
  2869.1 263.4 %reduce-scatter.32.cloned.1.call-done = f32[2752,512]{1,0:T(8,128)} async-done(((f32[2752,4096]{1,0:T(8,128)}), f32[2752,512]{1,0:T(8,128)}) %reduce-scatter.32.cloned.1.call-update) | async-done | bytes 5636112 | tf_op jit(solution)/shard_map/reduce_scatter | solution.py:266
  3132.6 120.4 %reduce-scatter.20.cloned.1.call-done = f32[512,1024]{1,0:T(8,128)} async-done(((f32[4096,1024]{1,0:T(8,128)}), f32[512,1024]{1,0:T(8,128)}) %reduce-scatter.20.cloned.1.call-update) | async-done | bytes 2097168 | tf_op jit(solution)/shard_map/reduce_scatter | solution.py:260
  3253.0 120.6 %reduce-scatter.22.cloned.1.call-done = f32[512,1024]{1,0:T(8,128)} async-done(((f32[4096,1024]{1,0:T(8,128)}), f32[512,1024]{1,0:T(8,128)}) %reduce-scatter.22.cloned.1.call-update) | async-done | bytes 2097168 | tf_op jit(solution)/shard_map/reduce_scatter | solution.py:261
  3373.5 120.4 %reduce-scatter.24.cloned.1.call-done = f32[512,1024]{1,0:T(8,128)} async-done(((f32[4096,1024]{1,0:T(8,128)}), f32[512,1024]{1,0:T(8,128)}) %reduce-scatter.24.cloned.1.call-update) | async-done | bytes 2097168 | tf_op jit(solution)/shard_map/reduce_scatter | solution.py:262
  3493.9 120.6 %reduce-scatter.26.cloned.1.call-done = f32[1024,512]{1,0:T(8,128)} async-done(((f32[1024,4096]{1,0:T(8,128)}), f32[1024,512]{1,0:T(8,128)}) %reduce-scatter.26.cloned.1.call-update) | async-done | bytes 2097168 | tf_op jit(solution)/shard_map/reduce_scatter | solution.py:263
  (372 shorter events, 650.1 us)
Async XLA Ops:
  7.2 158.8 %all-gather.11.cloned.1.call-start = ((), (), s32[]{:S(2)}) async-start(), calls=%async_computation.11 | async-start | bytes 10485760 | tf_op jit(solution)/shard_map/all_gather | solution.py:101
  13.5 207.0 %all-gather.13.cloned.1.call-start = ((), (), s32[]{:S(2)}) async-start(), calls=%async_computation.12 | async-start | bytes 9437184 | tf_op jit(solution)/shard_map/all_gather | solution.py:90
  14.2 262.6 %all-gather.15.cloned.1.call-start = ((), (), s32[]{:S(2)}) async-start(), calls=%async_computation.13 | async-start | bytes 9437184 | tf_op jit(solution)/shard_map/all_gather | solution.py:88
  15.0 318.0 %all-gather.17.cloned.1.call-start = ((), (), s32[]{:S(2)}) async-start(), calls=%async_computation.14 | async-start | bytes 9437184 | tf_op jit(solution)/shard_map/all_gather | solution.py:89
  15.6 375.2 %all-gather.19.cloned.1.call-start = ((), (), s32[]{:S(2)}) async-start(), calls=%async_computation.15 | async-start | bytes 9437184 | tf_op jit(solution)/shard_map/all_gather | solution.py:91
  16.1 669.9 %reduce-scatter.12.cloned.1.call-start = ((), (), s32[]{:S(2)}) async-start(), calls=%async_computation.16 | async-start | bytes 20971520 | tf_op jit(solution)/shard_map/reduce_scatter | solution.py:153
  405.6 475.7 %all-gather.23.cloned.1.call-start = ((), (), s32[]{:S(2)}) async-start(), calls=%async_computation.18 | async-start | bytes 25362432 | tf_op jit(solution)/shard_map/all_gather | solution.py:94
  406.4 570.4 %all-gather.21.cloned.1.call-start = ((), (), s32[]{:S(2)}) async-start(), calls=%async_computation.17 | async-start | bytes 10485760 | tf_op jit(solution)/shard_map/all_gather | solution.py:158
  692.8 402.8 %all-gather.25.cloned.1.call-start = ((), (), s32[]{:S(2)}) async-start(), calls=%async_computation.19 | async-start | bytes 25362432 | tf_op jit(solution)/shard_map/all_gather | solution.py:95
  693.5 522.7 %all-gather.27.cloned.1.call-start = ((), (), s32[]{:S(2)}) async-start(), calls=%async_computation.20 | async-start | bytes 25362432 | tf_op jit(solution)/shard_map/all_gather | solution.py:96
  694.1 902.3 %reduce-scatter.16.cloned.1.call-start = ((), (), s32[]{:S(2)}) async-start(), calls=%async_computation.22 | async-start | bytes 20971520 | tf_op jit(solution)/shard_map/reduce_scatter | solution.py:189
  695.1 49.1 %collective-permute-start = (bf16[256,4096]{1,0:T(8,128)(2,1)S(1)}, bf16[256,4096]{1,0:T(8,128)(2,1)S(1)}, u32[]{:S(2)}, u32[]{:S(2)}) collective-permute-start(bf16[256,4096]{1,0:T(8,128)(2,1)S(1)} %broadcast_multiply_fusion.1), channel_id=1, source_target_pairs={{0,1},{1,2},{2,3},{3,0},{4,5},{5,6},{6,7},{7,4},{8,9},{9,10},{10,1... | collective-permute-start | bytes 6291464 | tf_op jit(solution)/shard_map/ppermute | solution.py:175
  745.5 48.2 %collective-permute-start.1 = (bf16[256,4096]{1,0:T(8,128)(2,1)S(1)}, bf16[256,4096]{1,0:T(8,128)(2,1)}, u32[]{:S(2)}, u32[]{:S(2)}) collective-permute-start(bf16[256,4096]{1,0:T(8,128)(2,1)S(1)} %collective-permute-done), channel_id=1, source_target_pairs={{0,1},{1,2},{2,3},{3,0},{4,5},{5,6},{6,7},{7,4},{8,9},{9,10},{10,1... | collective-permute-start | bytes 6291464 | tf_op jit(solution)/shard_map/ppermute | solution.py:175
  793.7 68.0 %collective-permute-start.2 = (bf16[256,4096]{1,0:T(8,128)(2,1)}, bf16[256,4096]{1,0:T(8,128)(2,1)}, u32[]{:S(2)}, u32[]{:S(2)}) collective-permute-start(bf16[256,4096]{1,0:T(8,128)(2,1)} %collective-permute-done.1), channel_id=1, source_target_pairs={{0,1},{1,2},{2,3},{3,0},{4,5},{5,6},{6,7},{7,4},{8,9},{9,10},{10,1... | collective-permute-start | bytes 6291464 | tf_op jit(solution)/shard_map/ppermute | solution.py:175
  1316.0 442.1 %all-gather.29.cloned.1.call-start = ((), (), s32[]{:S(2)}) async-start(), calls=%async_computation.23 | async-start | bytes 10485760 | tf_op jit(solution)/shard_map/all_gather | solution.py:195
  1607.5 585.5 %reduce-scatter.18.cloned.1.call-start = ((), (), s32[]{:S(2)}) async-start(), calls=%async_computation.24 | async-start | bytes 20971520 | tf_op jit(solution)/shard_map/reduce_scatter | solution.py:251
  1914.3 427.2 %reduce-scatter.14.cloned.1.call-start = ((), (), s32[]{:S(2)}) async-start(), calls=%async_computation.21 | async-start | bytes 10485760 | tf_op jit(solution)/shard_map/reduce_scatter | solution.py:166
  1945.2 660.5 %reduce-scatter.28.cloned.1.call-start = ((), (), s32[]{:S(2)}) async-start(), calls=%async_computation.29 | async-start | bytes 50724864 | tf_op jit(solution)/shard_map/reduce_scatter | solution.py:264
  1977.1 892.1 %reduce-scatter.30.cloned.1.call-start = ((), (), s32[]{:S(2)}) async-start(), calls=%async_computation.30 | async-start | bytes 50724864 | tf_op jit(solution)/shard_map/reduce_scatter | solution.py:265
  2008.9 1123.7 %reduce-scatter.32.cloned.1.call-start = ((), (), s32[]{:S(2)}) async-start(), calls=%async_computation.31 | async-start | bytes 50724864 | tf_op jit(solution)/shard_map/reduce_scatter | solution.py:266
  2040.8 1212.2 %reduce-scatter.20.cloned.1.call-start = ((), (), s32[]{:S(2)}) async-start(), calls=%async_computation.25 | async-start | bytes 18874368 | tf_op jit(solution)/shard_map/reduce_scatter | solution.py:260
  2057.1 1316.4 %reduce-scatter.22.cloned.1.call-start = ((), (), s32[]{:S(2)}) async-start(), calls=%async_computation.26 | async-start | bytes 18874368 | tf_op jit(solution)/shard_map/reduce_scatter | solution.py:261
  2073.6 1420.4 %reduce-scatter.24.cloned.1.call-start = ((), (), s32[]{:S(2)}) async-start(), calls=%async_computation.27 | async-start | bytes 18874368 | tf_op jit(solution)/shard_map/reduce_scatter | solution.py:262
  2089.9 1524.6 %reduce-scatter.26.cloned.1.call-start = ((), (), s32[]{:S(2)}) async-start(), calls=%async_computation.28 | async-start | bytes 18874368 | tf_op jit(solution)/shard_map/reduce_scatter | solution.py:263
  (103 other events, 5087.2 us)
Sparse Core Ops, SparseCore 0:
  13.6 152.3 all-gather.10
  167.9 52.6 all-gather.12
  222.4 54.3 all-gather.14
  278.6 54.3 all-gather.16
  334.7 55.9 all-gather.18
  405.7 280.3 reduce-scatter.11
  688.1 119.3 all-gather.22
  809.7 166.9 all-gather.20
  978.8 116.8 all-gather.24
  1097.5 118.6 all-gather.26
  1316.1 280.2 reduce-scatter.15
  1607.6 150.3 all-gather.28
  1914.4 278.5 reduce-scatter.17
  2195.3 146.1 reduce-scatter.13
  2346.2 259.4 reduce-scatter.27
  2610.3 258.7 reduce-scatter.29
  2873.7 258.7 reduce-scatter.31
  3137.0 115.9 reduce-scatter.19
  3257.5 115.9 reduce-scatter.21
  3377.9 115.9 reduce-scatter.23
  3498.5 115.9 reduce-scatter.25
